TPU v7x, 128 devices: a whole 4x4x4 slice. The times are simulated.
128 devices in a mesh: az: 16 (over z, x_hi, core), dep: 8 (over y, x_lo).
Axes of the slice: x: 4 (x_hi: 2, x_lo: 2; x = x_hi * 2 + x_lo), y: 4, z: 4, core: 2. Of those that a mesh axis runs over, the one named last changes fastest.
Arguments:
- adjoint_in: float32 [2, 2048, 4096], P(None, 'az', 'dep'), may hold values from -6 to 6
- forward_field: float32 [8, 2, 2048, 4096], P(None, None, 'az', 'dep'), may hold values from -6 to 6
- screen: float32 [2048, 4096], P('az', 'dep'), may hold values from -3.140625 to 3.140625
- bed_weight: float32 [4096], replicated, may hold values from 0.1 to 1
- labels: int32 [2048, 32], P('az'), may hold values from 0 to 31
Outputs:
- adjoint_out: float32 [2, 2048, 4096], P(None, 'az', 'dep')
- sensitivity: float32 [32], replicated
All inputs are finite; a program needn't handle non-finite values.
Results may differ from a plain program's by a relative error of at most 0.0003.
Values sent between devices are 32-bit elements; how exact they have to be, the bound alone decides.
No kernel may reach another device: no remote copies, remote signals or barrier semaphores. Data moves between devices by JAX's collectives and lax.ppermute only.
A program may use at most 128 MiB of HBM per device.

v0:
```python
import math
import jax
import jax.numpy as jnp
from jax import lax
from jax.sharding import PartitionSpec as P

GROUPS = 32
coupling = 0.15
radix_rows = 64
label_block = 128
highest = lax.Precision.HIGHEST


def padded_2(cells, sides, width):
    for axis, dim in sides:
        count = lax.axis_size(axis)
        head = lax.slice_in_dim(cells, 0, width, axis=dim)
        tail = lax.slice_in_dim(cells, cells.shape[dim] - width, cells.shape[dim], axis=dim)
        cells = jnp.concatenate(
            [
                lax.ppermute(tail, axis, [(i, (i + 1) % count) for i in range(count)]),
                cells,
                lax.ppermute(head, axis, [((i + 1) % count, i) for i in range(count)]),
            ],
            axis=dim,
        )
    return cells


def angles(left, right, modulus, sign):
    product = left[:, None] * right[None, :] % modulus
    return sign * 2.0 * math.pi * product.astype(jnp.float32) / modulus


def combine(form, real_part, imag_part, cosine, sine):
    first = jnp.einsum(form, real_part, cosine, precision=highest) - jnp.einsum(
        form, imag_part, sine, precision=highest
    )
    second = jnp.einsum(form, real_part, sine, precision=highest) + jnp.einsum(
        form, imag_part, cosine, precision=highest
    )
    return (first, second)


def transform(real_part, imag_part, sign):
    length = real_part.shape[-1]
    second_len = length // radix_rows
    leading = real_part.shape[:-1]
    shaped_re = real_part.reshape(leading + (radix_rows, second_len))
    shaped_im = imag_part.reshape(leading + (radix_rows, second_len))
    outer_idx = jnp.arange(radix_rows, dtype=jnp.int32)
    inner_idx = jnp.arange(second_len, dtype=jnp.int32)
    first_ang = angles(outer_idx, outer_idx, radix_rows, sign)
    mid_re, mid_im = combine(
        "...ab,ac->...cb", shaped_re, shaped_im, jnp.cos(first_ang), jnp.sin(first_ang)
    )
    twist = angles(outer_idx, inner_idx, length, sign)
    twist_c = jnp.cos(twist)
    twist_s = jnp.sin(twist)
    mid_re, mid_im = (mid_re * twist_c - mid_im * twist_s, mid_re * twist_s + mid_im * twist_c)
    last_ang = angles(inner_idx, inner_idx, second_len, sign)
    out_re, out_im = combine(
        "...cb,bd->...dc", mid_re, mid_im, jnp.cos(last_ang), jnp.sin(last_ang)
    )
    return (out_re.reshape(leading + (length,)), out_im.reshape(leading + (length,)))


def propagate(field):
    length = field.shape[-1]
    freq = jnp.arange(length, dtype=jnp.int32)
    freq = jnp.where(freq < length // 2, freq, freq - length).astype(jnp.float32)
    beta = 30.0 * (freq / (length // 2)) ** 2
    spec_re, spec_im = transform(field[0], field[1], -1.0)
    cos_b = jnp.cos(beta)
    sin_b = jnp.sin(beta)
    turned_re = spec_re * cos_b - spec_im * sin_b
    turned_im = spec_re * sin_b + spec_im * cos_b
    back_re, back_im = transform(turned_re, turned_im, 1.0)
    return jnp.stack([back_re, back_im]) / length


def couple(padded):
    lap_wide = padded[:, :-2] + padded[:, 2:] - 2.0 * padded[:, 1:-1]
    lap = lap_wide[:, 1:-1]
    lap_two = lap_wide[:, :-2] + lap_wide[:, 2:] - 2.0 * lap
    centre = padded[:, 2:-2]
    half = 0.5 * coupling * coupling
    new_re = centre[0] + coupling * lap[1] - half * lap_two[0]
    new_im = centre[1] - coupling * lap[0] - half * lap_two[1]
    return jnp.stack([new_re, new_im])


def group_table(marks):
    return (marks[:, :, None] == jnp.arange(GROUPS, dtype=jnp.int32)[None, None, :]).astype(
        jnp.float32
    )


def group_terms(field, stored_step, weight, onehot):
    term = (field[1] * stored_step[0] - field[0] * stored_step[1]) * weight[None, :]
    blocks = term.reshape(term.shape[0], -1, label_block).sum(-1)
    return jnp.einsum("rb,rbg->g", blocks, onehot, precision=highest)


def rotate(field, cosine, sine):
    return jnp.stack([field[0] * cosine + field[1] * sine, field[1] * cosine - field[0] * sine])


def on_device(adjoint_in, forward_field, screen, bed_weight, labels):
    steps = forward_field.shape[0]
    dep_rank = lax.axis_index("dep")
    cols_here = adjoint_in.shape[2]
    count_blocks = cols_here // label_block
    sensitivity = jnp.zeros((GROUPS,), jnp.float32)
    field = adjoint_in
    weight_cols = lax.dynamic_slice_in_dim(bed_weight, dep_rank * cols_here, cols_here, 0)
    onehot_cols = group_table(
        lax.dynamic_slice_in_dim(labels, dep_rank * count_blocks, count_blocks, 1)
    )
    cosine = jnp.cos(screen)
    sine = jnp.sin(screen)
    for step in range(steps - 1, -1, -1):
        sensitivity = sensitivity + group_terms(
            field, forward_field[step], weight_cols, onehot_cols
        )
        padded = padded_2(rotate(field, cosine, sine), (("az", 1),), 2)
        deep = lax.all_to_all(couple(padded), "dep", split_axis=1, concat_axis=2, tiled=True)
        field = lax.all_to_all(propagate(deep), "dep", split_axis=2, concat_axis=1, tiled=True)
    total = lax.psum(sensitivity, ("az", "dep"))
    return (field, total)


def solution(mesh):
    return jax.shard_map(
        on_device,
        mesh=mesh,
        in_specs=(
            P(None, "az", "dep"),
            P(None, None, "az", "dep"),
            P("az", "dep"),
            P(),
            P("az", None),
        ),
        out_specs=(P(None, "az", "dep"), P()),
        check_vma=False,
    )
```

profile of v0, /device:TPU:1, one launch (start us, length us, event | category | flops | bytes accessed | tf_op | source)
XLA Modules:
  0.0 805.0 jit_solution(5096109944816775397)
XLA Ops:
  14.0 4.4 all-to-all-start
  19.6 6.2 all-to-all-done
  47.0 4.4 copy.132
  51.4 7.2 reshape.596
  58.6 10.0 %all_to_all.243 = f32[8,1,16384]{2,1,0:T(1,128)S(1)} all-to-all(f32[8,1,16384]{2,1,0:T(1,128)S(1)} %reshape.596), channel_id=1, replica_groups=mesh['az'=16,'dep'=8] {'dep'}, dimensions={0} | all-to-all | bytes 1048576 | tf_op jit(solution)/shard_map/all_to_all | solution.py:128
  70.8 7.5 reshape.597
  78.4 5.1 copy.133
  83.7 8.8 %collective-permute-start.3 = (f32[2,2,512]{2,1,0:T(2,128)S(1)}, f32[2,2,512]{2,1,0:T(2,128)S(1)}, u32[]{:S(2)}, u32[]{:S(2)}) collective-permute-start(f32[2,2,512]{2,1,0:T(2,128)S(1)} %get-tuple-element.107), channel_id=1, source_target_pairs={{8,0},{16,8},{24,16},{32,24},{40,32},{48,40},{56,48},{64,56},{72,6... | collective-permute-start | bytes 24584 | tf_op jit(solution)/shard_map/ppermute | solution.py:23
  96.7 10.0 %all_to_all.244 = f32[2,128,512]{2,0,1:T(2,128)S(1)} all-to-all(f32[2,128,512]{2,0,1:T(2,128)S(1)} %copy.134), channel_id=1, replica_groups=mesh['az'=16,'dep'=8] {'dep'}, dimensions={1} | all-to-all | bytes 1048576 | tf_op jit(solution)/shard_map/all_to_all | solution.py:127
  129.5 4.4 copy.136
  133.8 7.2 reshape.598
  141.1 10.0 %all_to_all.245 = f32[8,1,16384]{2,1,0:T(1,128)S(1)} all-to-all(f32[8,1,16384]{2,1,0:T(1,128)S(1)} %reshape.598), channel_id=1, replica_groups=mesh['az'=16,'dep'=8] {'dep'}, dimensions={0} | all-to-all | bytes 1048576 | tf_op jit(solution)/shard_map/all_to_all | solution.py:128
  152.8 7.5 reshape.599
  160.4 5.1 copy.137
  165.7 8.7 %collective-permute-start.5 = (f32[2,2,512]{2,1,0:T(2,128)S(1)}, f32[2,2,512]{2,1,0:T(2,128)S(1)}, u32[]{:S(2)}, u32[]{:S(2)}) collective-permute-start(f32[2,2,512]{2,1,0:T(2,128)S(1)} %get-tuple-element.101), channel_id=1, source_target_pairs={{8,0},{16,8},{24,16},{32,24},{40,32},{48,40},{56,48},{64,56},{72,6... | collective-permute-start | bytes 24584 | tf_op jit(solution)/shard_map/ppermute | solution.py:23
  178.4 10.0 %all_to_all.246 = f32[2,128,512]{2,0,1:T(2,128)S(1)} all-to-all(f32[2,128,512]{2,0,1:T(2,128)S(1)} %copy.138), channel_id=1, replica_groups=mesh['az'=16,'dep'=8] {'dep'}, dimensions={1} | all-to-all | bytes 1048576 | tf_op jit(solution)/shard_map/all_to_all | solution.py:127
  206.9 2.9 fusion.10
  216.5 4.4 copy.140
  220.9 7.2 reshape.600
  228.1 10.0 %all_to_all.247 = f32[8,1,16384]{2,1,0:T(1,128)S(1)} all-to-all(f32[8,1,16384]{2,1,0:T(1,128)S(1)} %reshape.600), channel_id=1, replica_groups=mesh['az'=16,'dep'=8] {'dep'}, dimensions={0} | all-to-all | bytes 1048576 | tf_op jit(solution)/shard_map/all_to_all | solution.py:128
  239.9 7.5 reshape.601
  247.4 5.1 copy.141
  252.7 8.7 %collective-permute-start.7 = (f32[2,2,512]{2,1,0:T(2,128)S(1)}, f32[2,2,512]{2,1,0:T(2,128)S(1)}, u32[]{:S(2)}, u32[]{:S(2)}) collective-permute-start(f32[2,2,512]{2,1,0:T(2,128)S(1)} %get-tuple-element.95), channel_id=1, source_target_pairs={{8,0},{16,8},{24,16},{32,24},{40,32},{48,40},{56,48},{64,56},{72,6... | collective-permute-start | bytes 24584 | tf_op jit(solution)/shard_map/ppermute | solution.py:23
  265.4 10.0 %all_to_all.248 = f32[2,128,512]{2,0,1:T(2,128)S(1)} all-to-all(f32[2,128,512]{2,0,1:T(2,128)S(1)} %copy.142), channel_id=1, replica_groups=mesh['az'=16,'dep'=8] {'dep'}, dimensions={1} | all-to-all | bytes 1048576 | tf_op jit(solution)/shard_map/all_to_all | solution.py:127
  301.4 3.6 fusion.9
  307.2 4.4 copy.144
  311.5 7.2 reshape.602
  318.8 10.0 %all_to_all.249 = f32[8,1,16384]{2,1,0:T(1,128)S(1)} all-to-all(f32[8,1,16384]{2,1,0:T(1,128)S(1)} %reshape.602), channel_id=1, replica_groups=mesh['az'=16,'dep'=8] {'dep'}, dimensions={0} | all-to-all | bytes 1048576 | tf_op jit(solution)/shard_map/all_to_all | solution.py:128
  330.5 7.5 reshape.603
  338.1 5.1 copy.145
  343.4 8.7 %collective-permute-start.9 = (f32[2,2,512]{2,1,0:T(2,128)S(1)}, f32[2,2,512]{2,1,0:T(2,128)S(1)}, u32[]{:S(2)}, u32[]{:S(2)}) collective-permute-start(f32[2,2,512]{2,1,0:T(2,128)S(1)} %get-tuple-element.89), channel_id=1, source_target_pairs={{8,0},{16,8},{24,16},{32,24},{40,32},{48,40},{56,48},{64,56},{72,6... | collective-permute-start | bytes 24584 | tf_op jit(solution)/shard_map/ppermute | solution.py:23
  356.4 10.0 %all_to_all.250 = f32[2,128,512]{2,0,1:T(2,128)S(1)} all-to-all(f32[2,128,512]{2,0,1:T(2,128)S(1)} %copy.146), channel_id=1, replica_groups=mesh['az'=16,'dep'=8] {'dep'}, dimensions={1} | all-to-all | bytes 1048576 | tf_op jit(solution)/shard_map/all_to_all | solution.py:127
  392.4 3.6 fusion.7
  398.2 4.4 copy.148
  402.5 7.2 reshape.604
  409.8 10.0 %all_to_all.251 = f32[8,1,16384]{2,1,0:T(1,128)S(1)} all-to-all(f32[8,1,16384]{2,1,0:T(1,128)S(1)} %reshape.604), channel_id=1, replica_groups=mesh['az'=16,'dep'=8] {'dep'}, dimensions={0} | all-to-all | bytes 1048576 | tf_op jit(solution)/shard_map/all_to_all | solution.py:128
  421.5 7.5 reshape.605
  429.1 5.1 copy.149
  434.4 8.6 %collective-permute-start.11 = (f32[2,2,512]{2,1,0:T(2,128)S(1)}, f32[2,2,512]{2,1,0:T(2,128)S(1)}, u32[]{:S(2)}, u32[]{:S(2)}) collective-permute-start(f32[2,2,512]{2,1,0:T(2,128)S(1)} %get-tuple-element.83), channel_id=1, source_target_pairs={{8,0},{16,8},{24,16},{32,24},{40,32},{48,40},{56,48},{64,56},{72,6... | collective-permute-start | bytes 24584 | tf_op jit(solution)/shard_map/ppermute | solution.py:23
  447.4 10.0 %all_to_all.252 = f32[2,128,512]{2,0,1:T(2,128)S(1)} all-to-all(f32[2,128,512]{2,0,1:T(2,128)S(1)} %copy.150), channel_id=1, replica_groups=mesh['az'=16,'dep'=8] {'dep'}, dimensions={1} | all-to-all | bytes 1048576 | tf_op jit(solution)/shard_map/all_to_all | solution.py:127
  483.5 3.6 fusion.5
  489.2 4.4 copy.152
  493.6 7.2 reshape.606
  500.8 10.0 %all_to_all.253 = f32[8,1,16384]{2,1,0:T(1,128)S(1)} all-to-all(f32[8,1,16384]{2,1,0:T(1,128)S(1)} %reshape.606), channel_id=1, replica_groups=mesh['az'=16,'dep'=8] {'dep'}, dimensions={0} | all-to-all | bytes 1048576 | tf_op jit(solution)/shard_map/all_to_all | solution.py:128
  512.6 7.5 reshape.607
  520.1 5.1 copy.153
  525.5 8.7 %collective-permute-start.13 = (f32[2,2,512]{2,1,0:T(2,128)S(1)}, f32[2,2,512]{2,1,0:T(2,128)S(1)}, u32[]{:S(2)}, u32[]{:S(2)}) collective-permute-start(f32[2,2,512]{2,1,0:T(2,128)S(1)} %get-tuple-element.77), channel_id=1, source_target_pairs={{8,0},{16,8},{24,16},{32,24},{40,32},{48,40},{56,48},{64,56},{72,6... | collective-permute-start | bytes 24584 | tf_op jit(solution)/shard_map/ppermute | solution.py:23
  538.5 10.0 %all_to_all.254 = f32[2,128,512]{2,0,1:T(2,128)S(1)} all-to-all(f32[2,128,512]{2,0,1:T(2,128)S(1)} %copy.154), channel_id=1, replica_groups=mesh['az'=16,'dep'=8] {'dep'}, dimensions={1} | all-to-all | bytes 1048576 | tf_op jit(solution)/shard_map/all_to_all | solution.py:127
  574.6 3.6 fusion.3
  580.3 4.4 copy.156
  584.7 7.9 reshape.608
  592.6 3.5 all-to-all-start.13
  597.6 4.2 fusion.951
  605.3 7.5 reshape.609
  612.9 5.1 copy.157
  618.2 8.5 %collective-permute-start.15 = (f32[2,2,512]{2,1,0:T(2,128)S(1)}, f32[2,2,512]{2,1,0:T(2,128)S(1)}, u32[]{:S(2)}, u32[]{:S(2)}) collective-permute-start(f32[2,2,512]{2,1,0:T(2,128)S(1)} %get-tuple-element.71), channel_id=1, source_target_pairs={{8,0},{16,8},{24,16},{32,24},{40,32},{48,40},{56,48},{64,56},{72,6... | collective-permute-start | bytes 24584 | tf_op jit(solution)/shard_map/ppermute | solution.py:23
  667.7 3.8 all-to-all-start.14
  671.5 3.4 multiply_reduce_fusion.6
  700.2 4.4 copy.160
  704.5 7.9 reshape.610
  712.4 5.1 all-to-all-start.15
  719.1 70.0 %psum.7 = f32[32]{0:T(128)} all-reduce(f32[32]{0:T(128)S(1)} %add_add_fusion), channel_id=1, replica_groups=mesh['az'=16,'dep'=8] {'az','dep'}, use_global_device_ids=true, to_apply=%region_8.9 | all-reduce | flops 32 | bytes 256 | tf_op jit(solution)/shard_map/psum | solution.py:129
  790.9 7.6 reshape.611
  798.5 6.3 copy.161
  (380 shorter events, 308.4 us)
Async XLA Ops:
  0.6 596.3 %copy-start = (f32[4096]{0:T(1024)S(1)}, f32[4096]{0:T(1024)}, u32[]{:S(2)}) copy-start(f32[4096]{0:T(1024)} %param.8) | copy-start | bytes 49156
  3.7 5.5 collective-permute-start.1
  5.2 6.7 collective-permute-start
  14.0 11.8 %all-to-all-start = ((f32[2,128,512]{2,0,1:T(2,128)}), f32[2,128,512]{2,0,1:T(2,128)S(1)}, u32[]{:S(2)}, u32[]{:S(2)}) async-start(f32[2,128,512]{2,0,1:T(2,128)} %pad_maximum_fusion.24), calls=%async_computation | async-start | bytes 1048576 | tf_op jit(solution)/shard_map/all_to_all | solution.py:127
  83.7 9.6 %collective-permute-start.3 = (f32[2,2,512]{2,1,0:T(2,128)S(1)}, f32[2,2,512]{2,1,0:T(2,128)S(1)}, u32[]{:S(2)}, u32[]{:S(2)}) collective-permute-start(f32[2,2,512]{2,1,0:T(2,128)S(1)} %get-tuple-element.107), channel_id=1, source_target_pairs={{8,0},{16,8},{24,16},{32,24},{40,32},{48,40},{56,48},{64,56},{72,6... | collective-permute-start | bytes 24584 | tf_op jit(solution)/shard_map/ppermute | solution.py:23
  92.5 3.3 collective-permute-start.2
  165.7 9.5 %collective-permute-start.5 = (f32[2,2,512]{2,1,0:T(2,128)S(1)}, f32[2,2,512]{2,1,0:T(2,128)S(1)}, u32[]{:S(2)}, u32[]{:S(2)}) collective-permute-start(f32[2,2,512]{2,1,0:T(2,128)S(1)} %get-tuple-element.101), channel_id=1, source_target_pairs={{8,0},{16,8},{24,16},{32,24},{40,32},{48,40},{56,48},{64,56},{72,6... | collective-permute-start | bytes 24584 | tf_op jit(solution)/shard_map/ppermute | solution.py:23
  174.3 3.2 collective-permute-start.4
  252.7 9.5 %collective-permute-start.7 = (f32[2,2,512]{2,1,0:T(2,128)S(1)}, f32[2,2,512]{2,1,0:T(2,128)S(1)}, u32[]{:S(2)}, u32[]{:S(2)}) collective-permute-start(f32[2,2,512]{2,1,0:T(2,128)S(1)} %get-tuple-element.95), channel_id=1, source_target_pairs={{8,0},{16,8},{24,16},{32,24},{40,32},{48,40},{56,48},{64,56},{72,6... | collective-permute-start | bytes 24584 | tf_op jit(solution)/shard_map/ppermute | solution.py:23
  261.4 3.1 collective-permute-start.6
  343.3 9.6 %copy-start.1 = (f32[1,8,16,512]{3,2,1,0:T(8,128)}, f32[1,8,16,512]{3,2,1,0:T(8,128)S(1)}, u32[]{:S(2)}) copy-start(f32[1,8,16,512]{3,2,1,0:T(8,128)S(1)} %get-tuple-element.91) | copy-start | bytes 786436
  343.3 9.6 %copy-start.3 = (f32[1,8,16,512]{3,2,1,0:T(8,128)}, f32[1,8,16,512]{3,2,1,0:T(8,128)S(1)}, u32[]{:S(2)}) copy-start(f32[1,8,16,512]{3,2,1,0:T(8,128)S(1)} %get-tuple-element.90) | copy-start | bytes 786436
  343.4 9.5 %collective-permute-start.9 = (f32[2,2,512]{2,1,0:T(2,128)S(1)}, f32[2,2,512]{2,1,0:T(2,128)S(1)}, u32[]{:S(2)}, u32[]{:S(2)}) collective-permute-start(f32[2,2,512]{2,1,0:T(2,128)S(1)} %get-tuple-element.89), channel_id=1, source_target_pairs={{8,0},{16,8},{24,16},{32,24},{40,32},{48,40},{56,48},{64,56},{72,6... | collective-permute-start | bytes 24584 | tf_op jit(solution)/shard_map/ppermute | solution.py:23
  352.1 3.4 collective-permute-start.8
  434.3 9.6 %copy-start.5 = (f32[1,8,16,512]{3,2,1,0:T(8,128)}, f32[1,8,16,512]{3,2,1,0:T(8,128)S(1)}, u32[]{:S(2)}) copy-start(f32[1,8,16,512]{3,2,1,0:T(8,128)S(1)} %get-tuple-element.85) | copy-start | bytes 786436
  434.3 9.6 %copy-start.7 = (f32[1,8,16,512]{3,2,1,0:T(8,128)}, f32[1,8,16,512]{3,2,1,0:T(8,128)S(1)}, u32[]{:S(2)}) copy-start(f32[1,8,16,512]{3,2,1,0:T(8,128)S(1)} %get-tuple-element.84) | copy-start | bytes 786436
  434.4 9.4 %collective-permute-start.11 = (f32[2,2,512]{2,1,0:T(2,128)S(1)}, f32[2,2,512]{2,1,0:T(2,128)S(1)}, u32[]{:S(2)}, u32[]{:S(2)}) collective-permute-start(f32[2,2,512]{2,1,0:T(2,128)S(1)} %get-tuple-element.83), channel_id=1, source_target_pairs={{8,0},{16,8},{24,16},{32,24},{40,32},{48,40},{56,48},{64,56},{72,6... | collective-permute-start | bytes 24584 | tf_op jit(solution)/shard_map/ppermute | solution.py:23
  443.0 3.5 collective-permute-start.10
  525.3 9.6 %copy-start.9 = (f32[1,8,16,512]{3,2,1,0:T(8,128)}, f32[1,8,16,512]{3,2,1,0:T(8,128)S(1)}, u32[]{:S(2)}) copy-start(f32[1,8,16,512]{3,2,1,0:T(8,128)S(1)} %get-tuple-element.79) | copy-start | bytes 786436
  525.3 9.6 %copy-start.11 = (f32[1,8,16,512]{3,2,1,0:T(8,128)}, f32[1,8,16,512]{3,2,1,0:T(8,128)S(1)}, u32[]{:S(2)}) copy-start(f32[1,8,16,512]{3,2,1,0:T(8,128)S(1)} %get-tuple-element.78) | copy-start | bytes 786436
  525.5 9.5 %collective-permute-start.13 = (f32[2,2,512]{2,1,0:T(2,128)S(1)}, f32[2,2,512]{2,1,0:T(2,128)S(1)}, u32[]{:S(2)}, u32[]{:S(2)}) collective-permute-start(f32[2,2,512]{2,1,0:T(2,128)S(1)} %get-tuple-element.77), channel_id=1, source_target_pairs={{8,0},{16,8},{24,16},{32,24},{40,32},{48,40},{56,48},{64,56},{72,6... | collective-permute-start | bytes 24584 | tf_op jit(solution)/shard_map/ppermute | solution.py:23
  534.1 3.5 collective-permute-start.12
  580.3 15.8 %copy-start.13 = (f32[2,128,512]{2,1,0:T(8,128)S(1)}, f32[2,128,512]{2,1,0:T(8,128)}, u32[]{:S(2)}) copy-start(f32[2,128,512]{2,1,0:T(8,128)} %param.5) | copy-start | bytes 1572868
  592.6 11.0 %all-to-all-start.13 = ((f32[8,1,16384]{2,1,0:T(1,128)}), f32[8,1,16384]{2,1,0:T(1,128)S(1)}, u32[]{:S(2)}, u32[]{:S(2)}) async-start(f32[8,1,16384]{2,1,0:T(1,128)} %reshape.608), calls=%async_computation.13 | async-start | bytes 1048576 | tf_op jit(solution)/shard_map/all_to_all | solution.py:128
  618.2 47.7 %collective-permute-start.15 = (f32[2,2,512]{2,1,0:T(2,128)S(1)}, f32[2,2,512]{2,1,0:T(2,128)S(1)}, u32[]{:S(2)}, u32[]{:S(2)}) collective-permute-start(f32[2,2,512]{2,1,0:T(2,128)S(1)} %get-tuple-element.71), channel_id=1, source_target_pairs={{8,0},{16,8},{24,16},{32,24},{40,32},{48,40},{56,48},{64,56},{72,6... | collective-permute-start | bytes 24584 | tf_op jit(solution)/shard_map/ppermute | solution.py:23
  626.7 39.2 %collective-permute-start.14 = (f32[2,2,512]{2,1,0:T(2,128)S(1)}, f32[2,2,512]{2,1,0:T(2,128)S(1)}, u32[]{:S(2)}, u32[]{:S(2)}) collective-permute-start(f32[2,2,512]{2,1,0:T(2,128)S(1)} %get-tuple-element.70), channel_id=1, source_target_pairs={{0,8},{8,16},{16,24},{24,32},{32,40},{40,48},{48,56},{56,64},{64,7... | collective-permute-start | bytes 24584 | tf_op jit(solution)/shard_map/ppermute | solution.py:21
  642.1 22.3 %copy-start.4 = (f32[1,8,16,512]{3,2,1,0:T(8,128)S(1)}, f32[1,8,16,512]{3,2,1,0:T(8,128)}, u32[]{:S(2)}) copy-start(f32[1,8,16,512]{3,2,1,0:T(8,128)} %copy-done.3) | copy-start | bytes 786436
  643.8 21.3 %copy-start.2 = (f32[1,8,16,512]{3,2,1,0:T(8,128)S(1)}, f32[1,8,16,512]{3,2,1,0:T(8,128)}, u32[]{:S(2)}) copy-start(f32[1,8,16,512]{3,2,1,0:T(8,128)} %copy-done.1) | copy-start | bytes 786436
  666.4 8.5 %copy-start.8 = (f32[1,8,16,512]{3,2,1,0:T(8,128)S(1)}, f32[1,8,16,512]{3,2,1,0:T(8,128)}, u32[]{:S(2)}) copy-start(f32[1,8,16,512]{3,2,1,0:T(8,128)} %copy-done.7) | copy-start | bytes 786436
  666.4 9.3 %copy-start.6 = (f32[1,8,16,512]{3,2,1,0:T(8,128)S(1)}, f32[1,8,16,512]{3,2,1,0:T(8,128)}, u32[]{:S(2)}) copy-start(f32[1,8,16,512]{3,2,1,0:T(8,128)} %copy-done.5) | copy-start | bytes 786436
  666.4 9.4 %copy-start.12 = (f32[1,8,16,512]{3,2,1,0:T(8,128)S(1)}, f32[1,8,16,512]{3,2,1,0:T(8,128)}, u32[]{:S(2)}) copy-start(f32[1,8,16,512]{3,2,1,0:T(8,128)} %copy-done.11) | copy-start | bytes 786436
  666.5 9.4 %copy-start.10 = (f32[1,8,16,512]{3,2,1,0:T(8,128)S(1)}, f32[1,8,16,512]{3,2,1,0:T(8,128)}, u32[]{:S(2)}) copy-start(f32[1,8,16,512]{3,2,1,0:T(8,128)} %copy-done.9) | copy-start | bytes 786436
  667.7 8.5 %copy-start.14 = (f32[128,4,128]{2,1,0:T(4,128)S(1)}, f32[128,4,128]{2,1,0:T(4,128)}, u32[]{:S(2)}) copy-start(f32[128,4,128]{2,1,0:T(4,128)} %squeeze.218) | copy-start | bytes 786436
  667.7 8.6 %copy-start.15 = (f32[128,4,128]{2,1,0:T(4,128)S(1)}, f32[128,4,128]{2,1,0:T(4,128)}, u32[]{:S(2)}) copy-start(f32[128,4,128]{2,1,0:T(4,128)} %squeeze.219) | copy-start | bytes 786436
  667.7 8.6 %copy-start.16 = (f32[128,4,128]{2,1,0:T(4,128)S(1)}, f32[128,4,128]{2,1,0:T(4,128)}, u32[]{:S(2)}) copy-start(f32[128,4,128]{2,1,0:T(4,128)} %squeeze.216) | copy-start | bytes 786436
  667.7 8.6 %copy-start.17 = (f32[128,4,128]{2,1,0:T(4,128)S(1)}, f32[128,4,128]{2,1,0:T(4,128)}, u32[]{:S(2)}) copy-start(f32[128,4,128]{2,1,0:T(4,128)} %squeeze.217) | copy-start | bytes 786436
  667.7 11.4 %all-to-all-start.14 = ((f32[2,128,512]{2,0,1:T(2,128)}), f32[2,128,512]{2,0,1:T(2,128)S(1)}, u32[]{:S(2)}, u32[]{:S(2)}) async-start(f32[2,128,512]{2,0,1:T(2,128)} %copy.158), calls=%async_computation.14 | async-start | bytes 1048576 | tf_op jit(solution)/shard_map/all_to_all | solution.py:127
  700.1 17.3 %copy-start.18 = (f32[128,4]{1,0:T(8,128)S(1)}, f32[128,4]{1,0:T(8,128)}, u32[]{:S(2)}) copy-start(f32[128,4]{1,0:T(8,128)} %get-tuple-element.13) | copy-start | bytes 6148
  700.1 17.3 %copy-start.19 = (f32[128,4]{1,0:T(8,128)S(1)}, f32[128,4]{1,0:T(8,128)}, u32[]{:S(2)}) copy-start(f32[128,4]{1,0:T(8,128)} %get-tuple-element.14) | copy-start | bytes 6148
  700.1 17.3 %copy-start.20 = (f32[128,4]{1,0:T(8,128)S(1)}, f32[128,4]{1,0:T(8,128)}, u32[]{:S(2)}) copy-start(f32[128,4]{1,0:T(8,128)} %get-tuple-element.15) | copy-start | bytes 6148
  700.1 17.3 %copy-start.21 = (f32[128,4]{1,0:T(8,128)S(1)}, f32[128,4]{1,0:T(8,128)}, u32[]{:S(2)}) copy-start(f32[128,4]{1,0:T(8,128)} %get-tuple-element.16) | copy-start | bytes 6148
  700.1 17.3 %copy-start.22 = (f32[128,4]{1,0:T(8,128)S(1)}, f32[128,4]{1,0:T(8,128)}, u32[]{:S(2)}) copy-start(f32[128,4]{1,0:T(8,128)} %get-tuple-element.17) | copy-start | bytes 6148
  700.2 17.3 %copy-start.23 = (s32[128,4]{1,0:T(8,128)S(1)}, s32[128,4]{1,0:T(8,128)}, u32[]{:S(2)}) copy-start(s32[128,4]{1,0:T(8,128)} %copy.162) | copy-start | bytes 6148
  712.4 76.7 %all-to-all-start.15 = ((f32[8,1,16384]{2,1,0:T(1,128)}), f32[8,1,16384]{2,1,0:T(1,128)S(1)}, u32[]{:S(2)}, u32[]{:S(2)}) async-start(f32[8,1,16384]{2,1,0:T(1,128)} %reshape.610), calls=%async_computation.15 | async-start | bytes 1048576 | tf_op jit(solution)/shard_map/all_to_all | solution.py:128
where the time goes:
time: 812 us; the launch traced here: 805 us
  local copies, waits for them, and re-layouts  281 us (35%)
  blocking collectives  189 us (23%)
  matrix products  183 us (23%)
  starting transfers between devices  82 us (10%)
  other arithmetic  36 us (4%)
  waiting for transfers between devices  31.1 us (4%)
    unnamed x64, local copies, waits for them, and re-layouts  120 us
    psum x1, blocking collectives, on_device(): total = lax.psum(sensitivity, ('az', 'dep'))  70 us
    ppermute x8, starting transfers between devices, padded_2(): lax.ppermute(head, axis, [((i + 1) % count, i) for i in range(count)])  62 us
    all_to_all x6, blocking collectives, on_device(): lax.all_to_all(propagate(deep), 'dep', split_axis=2, concat_axis=1, tiled...  59.7 us
    all_to_all x6, blocking collectives, on_device(): lax.all_to_all(couple(padded), 'dep', split_axis=1, concat_axis=2, tiled=...  59.7 us
    dot_general x32, matrix products, combine(): jnp.einsum(form, imag_part, cosine, precision=highest)  50 us
    dot_general x32, matrix products, combine(): jnp.einsum(form, imag_part, sine, precision=highest)  47.5 us
    dot_general x32, matrix products, combine(): jnp.einsum(form, real_part, cosine, precision=highest)  43 us
  transfers between devices with their start and end apart: 20, of which 16 were waited for; matrix products, arithmetic and copies ran while one was open for 7% of the time, Pallas kernels for 0%

commit v1 on v0

--- a/solution.py
+++ b/solution.py
@@ -126,7 +126,7 @@
         padded = padded_2(rotate(field, cosine, sine), (("az", 1),), 2)
         deep = lax.all_to_all(couple(padded), "dep", split_axis=1, concat_axis=2, tiled=True)
         field = lax.all_to_all(propagate(deep), "dep", split_axis=2, concat_axis=1, tiled=True)
-    total = lax.psum(sensitivity, ("az", "dep"))
+    total = lax.psum(lax.psum(sensitivity, "dep"), "az")
     return (field, total)
 
 

time: 812 us -> 799 us (0.984)
  blocking collectives: 189 us -> 176 us
    psum x1 -> x2, blocking collectives: 70 us -> 56.9 us  [on_device(): total = lax.psum(lax.psum(sensitivity, 'dep'), 'az')]
where the time goes in v1:
time: 799 us; the launch traced here: 792 us
  local copies, waits for them, and re-layouts  281 us (35%)
  matrix products  183 us (23%)
  blocking collectives  176 us (22%)
  starting transfers between devices  81.9 us (10%)
  other arithmetic  37 us (5%)
  waiting for transfers between devices  30.8 us (4%)
    unnamed x64, local copies, waits for them, and re-layouts  120 us
    ppermute x8, starting transfers between devices, padded_2(): lax.ppermute(head, axis, [((i + 1) % count, i) for i in range(count)])  61.9 us
    all_to_all x6, blocking collectives, on_device(): lax.all_to_all(propagate(deep), 'dep', split_axis=2, concat_axis=1, tiled...  59.7 us
    all_to_all x6, blocking collectives, on_device(): lax.all_to_all(couple(padded), 'dep', split_axis=1, concat_axis=2, tiled=...  59.7 us
    psum x2, blocking collectives, on_device(): total = lax.psum(lax.psum(sensitivity, 'dep'), 'az')  56.9 us
    dot_general x32, matrix products, combine(): jnp.einsum(form, imag_part, cosine, precision=highest)  50 us
    dot_general x32, matrix products, combine(): jnp.einsum(form, imag_part, sine, precision=highest)  47.5 us
    dot_general x32, matrix products, combine(): jnp.einsum(form, real_part, cosine, precision=highest)  42.9 us
  transfers between devices with their start and end apart: 20, of which 16 were waited for; matrix products, arithmetic and copies ran while one was open for 7% of the time, Pallas kernels for 0%

profile of v1, /device:TPU:1, one launch (start us, length us, event | category | flops | bytes accessed | tf_op | source)
XLA Modules:
  0.0 792.4 jit_solution(4335563932589360800)
XLA Ops:
  14.0 4.4 all-to-all-start
  19.6 6.2 all-to-all-done
  47.0 4.4 copy.132
  51.4 7.2 reshape.596
  58.6 10.0 %all_to_all.243 = f32[8,1,16384]{2,1,0:T(1,128)S(1)} all-to-all(f32[8,1,16384]{2,1,0:T(1,128)S(1)} %reshape.596), channel_id=1, replica_groups=mesh['az'=16,'dep'=8] {'dep'}, dimensions={0} | all-to-all | bytes 1048576 | tf_op jit(solution)/shard_map/all_to_all | solution.py:128
  71.0 7.5 reshape.597
  78.6 5.1 copy.133
  83.9 8.8 %collective-permute-start.3 = (f32[2,2,512]{2,1,0:T(2,128)S(1)}, f32[2,2,512]{2,1,0:T(2,128)S(1)}, u32[]{:S(2)}, u32[]{:S(2)}) collective-permute-start(f32[2,2,512]{2,1,0:T(2,128)S(1)} %get-tuple-element.107), channel_id=1, source_target_pairs={{8,0},{16,8},{24,16},{32,24},{40,32},{48,40},{56,48},{64,56},{72,6... | collective-permute-start | bytes 24584 | tf_op jit(solution)/shard_map/ppermute | solution.py:23
  96.9 10.0 %all_to_all.244 = f32[2,128,512]{2,0,1:T(2,128)S(1)} all-to-all(f32[2,128,512]{2,0,1:T(2,128)S(1)} %copy.134), channel_id=1, replica_groups=mesh['az'=16,'dep'=8] {'dep'}, dimensions={1} | all-to-all | bytes 1048576 | tf_op jit(solution)/shard_map/all_to_all | solution.py:127
  129.7 4.4 copy.136
  134.0 7.2 reshape.598
  141.2 10.0 %all_to_all.245 = f32[8,1,16384]{2,1,0:T(1,128)S(1)} all-to-all(f32[8,1,16384]{2,1,0:T(1,128)S(1)} %reshape.598), channel_id=1, replica_groups=mesh['az'=16,'dep'=8] {'dep'}, dimensions={0} | all-to-all | bytes 1048576 | tf_op jit(solution)/shard_map/all_to_all | solution.py:128
  153.1 7.5 reshape.599
  160.7 5.1 copy.137
  166.0 8.7 %collective-permute-start.5 = (f32[2,2,512]{2,1,0:T(2,128)S(1)}, f32[2,2,512]{2,1,0:T(2,128)S(1)}, u32[]{:S(2)}, u32[]{:S(2)}) collective-permute-start(f32[2,2,512]{2,1,0:T(2,128)S(1)} %get-tuple-element.101), channel_id=1, source_target_pairs={{8,0},{16,8},{24,16},{32,24},{40,32},{48,40},{56,48},{64,56},{72,6... | collective-permute-start | bytes 24584 | tf_op jit(solution)/shard_map/ppermute | solution.py:23
  178.8 10.0 %all_to_all.246 = f32[2,128,512]{2,0,1:T(2,128)S(1)} all-to-all(f32[2,128,512]{2,0,1:T(2,128)S(1)} %copy.138), channel_id=1, replica_groups=mesh['az'=16,'dep'=8] {'dep'}, dimensions={1} | all-to-all | bytes 1048576 | tf_op jit(solution)/shard_map/all_to_all | solution.py:127
  216.9 4.4 copy.140
  221.2 7.2 reshape.600
  228.4 10.0 %all_to_all.247 = f32[8,1,16384]{2,1,0:T(1,128)S(1)} all-to-all(f32[8,1,16384]{2,1,0:T(1,128)S(1)} %reshape.600), channel_id=1, replica_groups=mesh['az'=16,'dep'=8] {'dep'}, dimensions={0} | all-to-all | bytes 1048576 | tf_op jit(solution)/shard_map/all_to_all | solution.py:128
  240.3 7.5 reshape.601
  247.9 5.1 copy.141
  253.2 8.7 %collective-permute-start.7 = (f32[2,2,512]{2,1,0:T(2,128)S(1)}, f32[2,2,512]{2,1,0:T(2,128)S(1)}, u32[]{:S(2)}, u32[]{:S(2)}) collective-permute-start(f32[2,2,512]{2,1,0:T(2,128)S(1)} %get-tuple-element.95), channel_id=1, source_target_pairs={{8,0},{16,8},{24,16},{32,24},{40,32},{48,40},{56,48},{64,56},{72,6... | collective-permute-start | bytes 24584 | tf_op jit(solution)/shard_map/ppermute | solution.py:23
  265.8 10.0 %all_to_all.248 = f32[2,128,512]{2,0,1:T(2,128)S(1)} all-to-all(f32[2,128,512]{2,0,1:T(2,128)S(1)} %copy.142), channel_id=1, replica_groups=mesh['az'=16,'dep'=8] {'dep'}, dimensions={1} | all-to-all | bytes 1048576 | tf_op jit(solution)/shard_map/all_to_all | solution.py:127
  301.8 3.6 fusion.9
  307.5 4.4 copy.144
  311.9 7.2 reshape.602
  319.1 10.0 %all_to_all.249 = f32[8,1,16384]{2,1,0:T(1,128)S(1)} all-to-all(f32[8,1,16384]{2,1,0:T(1,128)S(1)} %reshape.602), channel_id=1, replica_groups=mesh['az'=16,'dep'=8] {'dep'}, dimensions={0} | all-to-all | bytes 1048576 | tf_op jit(solution)/shard_map/all_to_all | solution.py:128
  331.0 7.5 reshape.603
  338.6 5.1 copy.145
  343.9 8.5 %collective-permute-start.9 = (f32[2,2,512]{2,1,0:T(2,128)S(1)}, f32[2,2,512]{2,1,0:T(2,128)S(1)}, u32[]{:S(2)}, u32[]{:S(2)}) collective-permute-start(f32[2,2,512]{2,1,0:T(2,128)S(1)} %get-tuple-element.89), channel_id=1, source_target_pairs={{8,0},{16,8},{24,16},{32,24},{40,32},{48,40},{56,48},{64,56},{72,6... | collective-permute-start | bytes 24584 | tf_op jit(solution)/shard_map/ppermute | solution.py:23
  356.6 10.0 %all_to_all.250 = f32[2,128,512]{2,0,1:T(2,128)S(1)} all-to-all(f32[2,128,512]{2,0,1:T(2,128)S(1)} %copy.146), channel_id=1, replica_groups=mesh['az'=16,'dep'=8] {'dep'}, dimensions={1} | all-to-all | bytes 1048576 | tf_op jit(solution)/shard_map/all_to_all | solution.py:127
  392.6 3.6 fusion.7
  398.3 4.4 copy.148
  402.7 7.2 reshape.604
  409.9 10.0 %all_to_all.251 = f32[8,1,16384]{2,1,0:T(1,128)S(1)} all-to-all(f32[8,1,16384]{2,1,0:T(1,128)S(1)} %reshape.604), channel_id=1, replica_groups=mesh['az'=16,'dep'=8] {'dep'}, dimensions={0} | all-to-all | bytes 1048576 | tf_op jit(solution)/shard_map/all_to_all | solution.py:128
  421.8 7.5 reshape.605
  429.4 5.1 copy.149
  434.7 8.7 %collective-permute-start.11 = (f32[2,2,512]{2,1,0:T(2,128)S(1)}, f32[2,2,512]{2,1,0:T(2,128)S(1)}, u32[]{:S(2)}, u32[]{:S(2)}) collective-permute-start(f32[2,2,512]{2,1,0:T(2,128)S(1)} %get-tuple-element.83), channel_id=1, source_target_pairs={{8,0},{16,8},{24,16},{32,24},{40,32},{48,40},{56,48},{64,56},{72,6... | collective-permute-start | bytes 24584 | tf_op jit(solution)/shard_map/ppermute | solution.py:23
  447.7 10.0 %all_to_all.252 = f32[2,128,512]{2,0,1:T(2,128)S(1)} all-to-all(f32[2,128,512]{2,0,1:T(2,128)S(1)} %copy.150), channel_id=1, replica_groups=mesh['az'=16,'dep'=8] {'dep'}, dimensions={1} | all-to-all | bytes 1048576 | tf_op jit(solution)/shard_map/all_to_all | solution.py:127
  483.6 3.6 fusion.5
  489.4 4.4 copy.152
  493.8 7.2 reshape.606
  501.0 10.0 %all_to_all.253 = f32[8,1,16384]{2,1,0:T(1,128)S(1)} all-to-all(f32[8,1,16384]{2,1,0:T(1,128)S(1)} %reshape.606), channel_id=1, replica_groups=mesh['az'=16,'dep'=8] {'dep'}, dimensions={0} | all-to-all | bytes 1048576 | tf_op jit(solution)/shard_map/all_to_all | solution.py:128
  512.9 7.5 reshape.607
  520.4 5.1 copy.153
  525.8 8.7 %collective-permute-start.13 = (f32[2,2,512]{2,1,0:T(2,128)S(1)}, f32[2,2,512]{2,1,0:T(2,128)S(1)}, u32[]{:S(2)}, u32[]{:S(2)}) collective-permute-start(f32[2,2,512]{2,1,0:T(2,128)S(1)} %get-tuple-element.77), channel_id=1, source_target_pairs={{8,0},{16,8},{24,16},{32,24},{40,32},{48,40},{56,48},{64,56},{72,6... | collective-permute-start | bytes 24584 | tf_op jit(solution)/shard_map/ppermute | solution.py:23
  538.8 10.0 %all_to_all.254 = f32[2,128,512]{2,0,1:T(2,128)S(1)} all-to-all(f32[2,128,512]{2,0,1:T(2,128)S(1)} %copy.154), channel_id=1, replica_groups=mesh['az'=16,'dep'=8] {'dep'}, dimensions={1} | all-to-all | bytes 1048576 | tf_op jit(solution)/shard_map/all_to_all | solution.py:127
  574.8 3.6 fusion.3
  580.6 4.4 copy.156
  585.0 7.9 reshape.608
  592.9 3.5 all-to-all-start.13
  597.9 4.2 fusion.951
  605.8 7.5 reshape.609
  613.3 5.1 copy.157
  618.6 8.5 %collective-permute-start.15 = (f32[2,2,512]{2,1,0:T(2,128)S(1)}, f32[2,2,512]{2,1,0:T(2,128)S(1)}, u32[]{:S(2)}, u32[]{:S(2)}) collective-permute-start(f32[2,2,512]{2,1,0:T(2,128)S(1)} %get-tuple-element.71), channel_id=1, source_target_pairs={{8,0},{16,8},{24,16},{32,24},{40,32},{48,40},{56,48},{64,56},{72,6... | collective-permute-start | bytes 24584 | tf_op jit(solution)/shard_map/ppermute | solution.py:23
  668.1 3.8 all-to-all-start.14
  672.0 3.4 multiply_reduce_fusion.6
  700.6 4.4 copy.160
  704.9 7.9 reshape.610
  712.8 5.1 all-to-all-start.15
  719.5 16.3 %psum.14 = f32[32]{0:T(128)S(1)} all-reduce(f32[32]{0:T(128)S(1)} %add_add_fusion), channel_id=1, replica_groups=mesh['az'=16,'dep'=8] {'dep'}, use_global_device_ids=true, to_apply=%region_8.9 | all-reduce | flops 32 | bytes 256 | tf_op jit(solution)/shard_map/psum | solution.py:129
  735.9 40.6 %psum.15 = f32[32]{0:T(128)} all-reduce(f32[32]{0:T(128)S(1)} %psum.14), channel_id=1, replica_groups=mesh['az'=16,'dep'=8] {'az'}, use_global_device_ids=true, to_apply=%region_9.10 | all-reduce | flops 32 | bytes 256 | tf_op jit(solution)/shard_map/psum | solution.py:129
  778.3 7.6 reshape.611
  785.9 6.3 copy.161
  (381 shorter events, 312.1 us)
Async XLA Ops:
  0.6 596.6 %copy-start = (f32[4096]{0:T(1024)S(1)}, f32[4096]{0:T(1024)}, u32[]{:S(2)}) copy-start(f32[4096]{0:T(1024)} %param.8) | copy-start | bytes 49156
  3.7 5.5 collective-permute-start.1
  5.2 6.7 collective-permute-start
  14.0 11.8 %all-to-all-start = ((f32[2,128,512]{2,0,1:T(2,128)}), f32[2,128,512]{2,0,1:T(2,128)S(1)}, u32[]{:S(2)}, u32[]{:S(2)}) async-start(f32[2,128,512]{2,0,1:T(2,128)} %pad_maximum_fusion.24), calls=%async_computation | async-start | bytes 1048576 | tf_op jit(solution)/shard_map/all_to_all | solution.py:127
  83.9 9.6 %collective-permute-start.3 = (f32[2,2,512]{2,1,0:T(2,128)S(1)}, f32[2,2,512]{2,1,0:T(2,128)S(1)}, u32[]{:S(2)}, u32[]{:S(2)}) collective-permute-start(f32[2,2,512]{2,1,0:T(2,128)S(1)} %get-tuple-element.107), channel_id=1, source_target_pairs={{8,0},{16,8},{24,16},{32,24},{40,32},{48,40},{56,48},{64,56},{72,6... | collective-permute-start | bytes 24584 | tf_op jit(solution)/shard_map/ppermute | solution.py:23
  92.7 3.3 collective-permute-start.2
  166.0 9.5 %collective-permute-start.5 = (f32[2,2,512]{2,1,0:T(2,128)S(1)}, f32[2,2,512]{2,1,0:T(2,128)S(1)}, u32[]{:S(2)}, u32[]{:S(2)}) collective-permute-start(f32[2,2,512]{2,1,0:T(2,128)S(1)} %get-tuple-element.101), channel_id=1, source_target_pairs={{8,0},{16,8},{24,16},{32,24},{40,32},{48,40},{56,48},{64,56},{72,6... | collective-permute-start | bytes 24584 | tf_op jit(solution)/shard_map/ppermute | solution.py:23
  174.6 3.2 collective-permute-start.4
  253.2 9.5 %collective-permute-start.7 = (f32[2,2,512]{2,1,0:T(2,128)S(1)}, f32[2,2,512]{2,1,0:T(2,128)S(1)}, u32[]{:S(2)}, u32[]{:S(2)}) collective-permute-start(f32[2,2,512]{2,1,0:T(2,128)S(1)} %get-tuple-element.95), channel_id=1, source_target_pairs={{8,0},{16,8},{24,16},{32,24},{40,32},{48,40},{56,48},{64,56},{72,6... | collective-permute-start | bytes 24584 | tf_op jit(solution)/shard_map/ppermute | solution.py:23
  261.8 3.0 collective-permute-start.6
  343.7 9.5 %copy-start.1 = (f32[1,8,16,512]{3,2,1,0:T(8,128)}, f32[1,8,16,512]{3,2,1,0:T(8,128)S(1)}, u32[]{:S(2)}) copy-start(f32[1,8,16,512]{3,2,1,0:T(8,128)S(1)} %get-tuple-element.91) | copy-start | bytes 786436
  343.8 9.5 %copy-start.3 = (f32[1,8,16,512]{3,2,1,0:T(8,128)}, f32[1,8,16,512]{3,2,1,0:T(8,128)S(1)}, u32[]{:S(2)}) copy-start(f32[1,8,16,512]{3,2,1,0:T(8,128)S(1)} %get-tuple-element.90) | copy-start | bytes 786436
  343.9 9.3 %collective-permute-start.9 = (f32[2,2,512]{2,1,0:T(2,128)S(1)}, f32[2,2,512]{2,1,0:T(2,128)S(1)}, u32[]{:S(2)}, u32[]{:S(2)}) collective-permute-start(f32[2,2,512]{2,1,0:T(2,128)S(1)} %get-tuple-element.89), channel_id=1, source_target_pairs={{8,0},{16,8},{24,16},{32,24},{40,32},{48,40},{56,48},{64,56},{72,6... | collective-permute-start | bytes 24584 | tf_op jit(solution)/shard_map/ppermute | solution.py:23
  352.4 3.3 collective-permute-start.8
  434.5 9.6 %copy-start.5 = (f32[1,8,16,512]{3,2,1,0:T(8,128)}, f32[1,8,16,512]{3,2,1,0:T(8,128)S(1)}, u32[]{:S(2)}) copy-start(f32[1,8,16,512]{3,2,1,0:T(8,128)S(1)} %get-tuple-element.85) | copy-start | bytes 786436
  434.6 9.6 %copy-start.7 = (f32[1,8,16,512]{3,2,1,0:T(8,128)}, f32[1,8,16,512]{3,2,1,0:T(8,128)S(1)}, u32[]{:S(2)}) copy-start(f32[1,8,16,512]{3,2,1,0:T(8,128)S(1)} %get-tuple-element.84) | copy-start | bytes 786436
  434.7 9.5 %collective-permute-start.11 = (f32[2,2,512]{2,1,0:T(2,128)S(1)}, f32[2,2,512]{2,1,0:T(2,128)S(1)}, u32[]{:S(2)}, u32[]{:S(2)}) collective-permute-start(f32[2,2,512]{2,1,0:T(2,128)S(1)} %get-tuple-element.83), channel_id=1, source_target_pairs={{8,0},{16,8},{24,16},{32,24},{40,32},{48,40},{56,48},{64,56},{72,6... | collective-permute-start | bytes 24584 | tf_op jit(solution)/shard_map/ppermute | solution.py:23
  443.3 3.4 collective-permute-start.10
  525.6 9.6 %copy-start.9 = (f32[1,8,16,512]{3,2,1,0:T(8,128)}, f32[1,8,16,512]{3,2,1,0:T(8,128)S(1)}, u32[]{:S(2)}) copy-start(f32[1,8,16,512]{3,2,1,0:T(8,128)S(1)} %get-tuple-element.79) | copy-start | bytes 786436
  525.6 9.6 %copy-start.11 = (f32[1,8,16,512]{3,2,1,0:T(8,128)}, f32[1,8,16,512]{3,2,1,0:T(8,128)S(1)}, u32[]{:S(2)}) copy-start(f32[1,8,16,512]{3,2,1,0:T(8,128)S(1)} %get-tuple-element.78) | copy-start | bytes 786436
  525.8 9.5 %collective-permute-start.13 = (f32[2,2,512]{2,1,0:T(2,128)S(1)}, f32[2,2,512]{2,1,0:T(2,128)S(1)}, u32[]{:S(2)}, u32[]{:S(2)}) collective-permute-start(f32[2,2,512]{2,1,0:T(2,128)S(1)} %get-tuple-element.77), channel_id=1, source_target_pairs={{8,0},{16,8},{24,16},{32,24},{40,32},{48,40},{56,48},{64,56},{72,6... | collective-permute-start | bytes 24584 | tf_op jit(solution)/shard_map/ppermute | solution.py:23
  534.4 3.5 collective-permute-start.12
  580.6 15.8 %copy-start.13 = (f32[2,128,512]{2,1,0:T(8,128)S(1)}, f32[2,128,512]{2,1,0:T(8,128)}, u32[]{:S(2)}) copy-start(f32[2,128,512]{2,1,0:T(8,128)} %param.5) | copy-start | bytes 1572868
  592.9 11.0 %all-to-all-start.13 = ((f32[8,1,16384]{2,1,0:T(1,128)}), f32[8,1,16384]{2,1,0:T(1,128)S(1)}, u32[]{:S(2)}, u32[]{:S(2)}) async-start(f32[8,1,16384]{2,1,0:T(1,128)} %reshape.608), calls=%async_computation.13 | async-start | bytes 1048576 | tf_op jit(solution)/shard_map/all_to_all | solution.py:128
  618.6 47.7 %collective-permute-start.15 = (f32[2,2,512]{2,1,0:T(2,128)S(1)}, f32[2,2,512]{2,1,0:T(2,128)S(1)}, u32[]{:S(2)}, u32[]{:S(2)}) collective-permute-start(f32[2,2,512]{2,1,0:T(2,128)S(1)} %get-tuple-element.71), channel_id=1, source_target_pairs={{8,0},{16,8},{24,16},{32,24},{40,32},{48,40},{56,48},{64,56},{72,6... | collective-permute-start | bytes 24584 | tf_op jit(solution)/shard_map/ppermute | solution.py:23
  627.1 39.2 %collective-permute-start.14 = (f32[2,2,512]{2,1,0:T(2,128)S(1)}, f32[2,2,512]{2,1,0:T(2,128)S(1)}, u32[]{:S(2)}, u32[]{:S(2)}) collective-permute-start(f32[2,2,512]{2,1,0:T(2,128)S(1)} %get-tuple-element.70), channel_id=1, source_target_pairs={{0,8},{8,16},{16,24},{24,32},{32,40},{40,48},{48,56},{56,64},{64,7... | collective-permute-start | bytes 24584 | tf_op jit(solution)/shard_map/ppermute | solution.py:21
  642.5 22.3 %copy-start.4 = (f32[1,8,16,512]{3,2,1,0:T(8,128)S(1)}, f32[1,8,16,512]{3,2,1,0:T(8,128)}, u32[]{:S(2)}) copy-start(f32[1,8,16,512]{3,2,1,0:T(8,128)} %copy-done.3) | copy-start | bytes 786436
  644.3 21.3 %copy-start.2 = (f32[1,8,16,512]{3,2,1,0:T(8,128)S(1)}, f32[1,8,16,512]{3,2,1,0:T(8,128)}, u32[]{:S(2)}) copy-start(f32[1,8,16,512]{3,2,1,0:T(8,128)} %copy-done.1) | copy-start | bytes 786436
  666.8 8.5 %copy-start.8 = (f32[1,8,16,512]{3,2,1,0:T(8,128)S(1)}, f32[1,8,16,512]{3,2,1,0:T(8,128)}, u32[]{:S(2)}) copy-start(f32[1,8,16,512]{3,2,1,0:T(8,128)} %copy-done.7) | copy-start | bytes 786436
  666.9 9.3 %copy-start.6 = (f32[1,8,16,512]{3,2,1,0:T(8,128)S(1)}, f32[1,8,16,512]{3,2,1,0:T(8,128)}, u32[]{:S(2)}) copy-start(f32[1,8,16,512]{3,2,1,0:T(8,128)} %copy-done.5) | copy-start | bytes 786436
  666.9 9.4 %copy-start.12 = (f32[1,8,16,512]{3,2,1,0:T(8,128)S(1)}, f32[1,8,16,512]{3,2,1,0:T(8,128)}, u32[]{:S(2)}) copy-start(f32[1,8,16,512]{3,2,1,0:T(8,128)} %copy-done.11) | copy-start | bytes 786436
  666.9 9.4 %copy-start.10 = (f32[1,8,16,512]{3,2,1,0:T(8,128)S(1)}, f32[1,8,16,512]{3,2,1,0:T(8,128)}, u32[]{:S(2)}) copy-start(f32[1,8,16,512]{3,2,1,0:T(8,128)} %copy-done.9) | copy-start | bytes 786436
  668.1 8.5 %copy-start.14 = (f32[128,4,128]{2,1,0:T(4,128)S(1)}, f32[128,4,128]{2,1,0:T(4,128)}, u32[]{:S(2)}) copy-start(f32[128,4,128]{2,1,0:T(4,128)} %squeeze.218) | copy-start | bytes 786436
  668.1 8.6 %copy-start.15 = (f32[128,4,128]{2,1,0:T(4,128)S(1)}, f32[128,4,128]{2,1,0:T(4,128)}, u32[]{:S(2)}) copy-start(f32[128,4,128]{2,1,0:T(4,128)} %squeeze.219) | copy-start | bytes 786436
  668.1 8.6 %copy-start.16 = (f32[128,4,128]{2,1,0:T(4,128)S(1)}, f32[128,4,128]{2,1,0:T(4,128)}, u32[]{:S(2)}) copy-start(f32[128,4,128]{2,1,0:T(4,128)} %squeeze.216) | copy-start | bytes 786436
  668.1 8.6 %copy-start.17 = (f32[128,4,128]{2,1,0:T(4,128)S(1)}, f32[128,4,128]{2,1,0:T(4,128)}, u32[]{:S(2)}) copy-start(f32[128,4,128]{2,1,0:T(4,128)} %squeeze.217) | copy-start | bytes 786436
  668.1 11.4 %all-to-all-start.14 = ((f32[2,128,512]{2,0,1:T(2,128)}), f32[2,128,512]{2,0,1:T(2,128)S(1)}, u32[]{:S(2)}, u32[]{:S(2)}) async-start(f32[2,128,512]{2,0,1:T(2,128)} %copy.158), calls=%async_computation.14 | async-start | bytes 1048576 | tf_op jit(solution)/shard_map/all_to_all | solution.py:127
  700.5 17.4 %copy-start.18 = (f32[128,4]{1,0:T(8,128)S(1)}, f32[128,4]{1,0:T(8,128)}, u32[]{:S(2)}) copy-start(f32[128,4]{1,0:T(8,128)} %get-tuple-element.13) | copy-start | bytes 6148
  700.5 17.4 %copy-start.19 = (f32[128,4]{1,0:T(8,128)S(1)}, f32[128,4]{1,0:T(8,128)}, u32[]{:S(2)}) copy-start(f32[128,4]{1,0:T(8,128)} %get-tuple-element.14) | copy-start | bytes 6148
  700.5 17.4 %copy-start.20 = (f32[128,4]{1,0:T(8,128)S(1)}, f32[128,4]{1,0:T(8,128)}, u32[]{:S(2)}) copy-start(f32[128,4]{1,0:T(8,128)} %get-tuple-element.15) | copy-start | bytes 6148
  700.6 17.4 %copy-start.21 = (f32[128,4]{1,0:T(8,128)S(1)}, f32[128,4]{1,0:T(8,128)}, u32[]{:S(2)}) copy-start(f32[128,4]{1,0:T(8,128)} %get-tuple-element.16) | copy-start | bytes 6148
  700.6 17.4 %copy-start.22 = (f32[128,4]{1,0:T(8,128)S(1)}, f32[128,4]{1,0:T(8,128)}, u32[]{:S(2)}) copy-start(f32[128,4]{1,0:T(8,128)} %get-tuple-element.17) | copy-start | bytes 6148
  700.6 17.4 %copy-start.23 = (s32[128,4]{1,0:T(8,128)S(1)}, s32[128,4]{1,0:T(8,128)}, u32[]{:S(2)}) copy-start(s32[128,4]{1,0:T(8,128)} %copy.162) | copy-start | bytes 6148
  712.8 63.6 %all-to-all-start.15 = ((f32[8,1,16384]{2,1,0:T(1,128)}), f32[8,1,16384]{2,1,0:T(1,128)S(1)}, u32[]{:S(2)}, u32[]{:S(2)}) async-start(f32[8,1,16384]{2,1,0:T(1,128)} %reshape.610), calls=%async_computation.15 | async-start | bytes 1048576 | tf_op jit(solution)/shard_map/all_to_all | solution.py:128
